TPU v7x, 128 devices: a whole 4x4x4 slice. The times are simulated.
128 devices in a mesh: clip: 8 (over x, core), tok: 16 (over y, z).
Axes of the slice: x: 4, y: 4, z: 4, core: 2. Of those that a mesh axis runs over, the one named last changes fastest.
Arguments:
- tokens: bfloat16 [65536, 1024], P(('clip', 'tok')), may hold values from -80 to 80
- slot_keys: bfloat16 [1024, 1024], replicated, may hold values from -64 to 64
- w_in: bfloat16 [16, 1024, 4096], P('tok', None, 'clip'), may hold values from -0.1875 to 0.1875
- w_back: bfloat16 [16, 4096, 1024], P('tok', 'clip'), may hold values from -0.09375 to 0.09375
- w_proj: bfloat16 [1024, 512], replicated, may hold values from -0.1875 to 0.1875
- dec_source: int32 [8, 4096], P('clip'), may hold values from 0 to 8192, as said below
- mask_token: bfloat16 [512], replicated, may hold values from -80 to 80
- w_qkv: bfloat16 [512, 1536], replicated, may hold values from -8 to 8
- w_out: bfloat16 [512, 512], replicated, may hold values from -9 to 9
Outputs:
- decoded: bfloat16 [32768, 512], P(('clip', 'tok'))
Inputs may be any that keep to these rules, and one draw needn't show every extreme that they name: `dec_source`: within a clip no visible index appears twice. For each aligned block of 256 decoder positions and each aligned block of 512 visible tokens, at most 16 positions of the first show tokens of the second, and some pair of blocks reaches 16 in every clip.
All inputs are finite; a program needn't handle non-finite values.
Results may differ from a plain program's by a relative error of at most 0.025.
Values may be sent and summed in bfloat16 or wider, within the bound.
A program may use at most 64 MiB of HBM per device.

v0:
```python
import math
import jax
import jax.numpy as jnp
from jax import lax
from jax.sharding import PartitionSpec as P

HEADS = 16


def layer_norm(values):
    centre = values - jnp.mean(values, axis=-1, keepdims=True)
    spread = jnp.mean(centre * centre, axis=-1, keepdims=True)
    return centre * lax.rsqrt(spread + 1e-05)


def sinusoid(places, width):
    half = width // 2
    speeds = jnp.exp(-math.log(10000.0) * jnp.arange(half).astype(jnp.float32) / half)
    angles = places.astype(jnp.float32)[:, None] * speeds[None, :]
    return jnp.concatenate([jnp.sin(angles), jnp.cos(angles)], axis=1)


def attend(queries, key_rows, value_rows):
    heads_here, head_dim, count = queries.shape
    block = math.gcd(count, 512)
    scale = 1.0 / math.sqrt(head_dim)
    blocks = queries.reshape(heads_here, head_dim, count // block, block).transpose(2, 0, 1, 3)

    def one_block(query_block):
        scores = (
            jnp.einsum("hkq,hkn->hqn", query_block, key_rows, preferred_element_type=jnp.float32)
            * scale
        )
        highest = jnp.max(scores, axis=-1)
        raised = jnp.exp(scores - highest[..., None]).astype(jnp.bfloat16)
        totals = jnp.sum(raised.astype(jnp.float32), axis=-1)
        summed = jnp.einsum("hqn,hkn->hkq", raised, value_rows, preferred_element_type=jnp.float32)
        return (summed / totals[:, None, :]).astype(jnp.bfloat16)

    outcome = lax.map(one_block, blocks)
    return outcome.transpose(1, 2, 0, 3).reshape(heads_here, head_dim, count)


def per_device(tokens, slot_keys, w_in, w_back, w_proj, dec_source, mask_token, w_qkv, w_out):
    vis_dev, width = tokens.shape
    n_tok = lax.axis_size("tok")
    dec_width = w_proj.shape[1]
    normed = layer_norm(tokens.astype(jnp.float32)).astype(jnp.bfloat16)
    logits = jnp.dot(normed, slot_keys, preferred_element_type=jnp.float32)
    col_top = lax.pmax(jnp.max(logits, axis=0), "tok")
    dispatch = jnp.exp(logits - col_top[None, :]).astype(jnp.bfloat16)
    slot_sums = lax.dot_general(
        dispatch, normed, (((0,), (0,)), ((), ())), preferred_element_type=jnp.float32
    )
    slot_totals = jnp.sum(dispatch.astype(jnp.float32), axis=0)
    mine_sums, mine_totals = (
        lax.psum_scatter(slot_sums, "tok", scatter_dimension=0, tiled=True),
        lax.psum_scatter(slot_totals, "tok", scatter_dimension=0, tiled=True),
    )
    slot_in = (mine_sums / mine_totals[:, None]).astype(jnp.bfloat16)
    first_proj = w_in[0]
    second_proj = w_back[0]
    hidden = jax.nn.gelu(
        jnp.dot(
            lax.all_gather(slot_in, "clip", axis=0, tiled=True),
            first_proj,
            preferred_element_type=jnp.float32,
        )
    ).astype(jnp.bfloat16)
    partial_out = jnp.dot(hidden, second_proj, preferred_element_type=jnp.float32)
    slot_out = lax.psum_scatter(partial_out, "clip", scatter_dimension=0, tiled=True).astype(
        jnp.bfloat16
    )
    row_top = jnp.max(logits, axis=1, keepdims=True)
    raised = jnp.exp(logits - row_top)
    combine = (raised / jnp.sum(raised, axis=1, keepdims=True)).astype(jnp.bfloat16)
    moe = jnp.dot(
        combine,
        lax.all_gather(slot_out, "tok", axis=0, tiled=True),
        preferred_element_type=jnp.float32,
    ).astype(jnp.bfloat16)
    projected = jnp.dot(moe, w_proj, preferred_element_type=jnp.float32).astype(jnp.bfloat16)
    listing = dec_source[0]
    dec_total = listing.shape[0]
    dec_dev = dec_total // n_tok
    vis_all = vis_dev * n_tok
    myself = lax.axis_index("tok")
    own_list = lax.dynamic_slice_in_dim(listing, myself * dec_dev, dec_dev)
    visible = own_list < vis_all
    places = myself * dec_dev + jnp.arange(dec_dev)
    filler = (mask_token.astype(jnp.float32)[None, :] + sinusoid(places, dec_width)).astype(
        jnp.bfloat16
    )
    everyone = lax.all_gather(projected, "tok", axis=0, tiled=True)
    picked = jnp.take(everyone, jnp.minimum(own_list, vis_all - 1), axis=0)
    dec_in = jnp.where(visible[:, None], picked, filler)
    head_dim = dec_width // HEADS
    dec_normed = layer_norm(dec_in.astype(jnp.float32)).astype(jnp.bfloat16)
    qkv = jnp.einsum(
        "pd,dchk->chkp",
        dec_normed,
        w_qkv.reshape(dec_width, 3, HEADS, head_dim),
        preferred_element_type=jnp.float32,
    ).astype(jnp.bfloat16)
    spread = lax.all_to_all(qkv, "tok", split_axis=1, concat_axis=3, tiled=True)
    attended = attend(spread[0], spread[1], spread[2])
    attended = lax.all_to_all(attended, "tok", split_axis=2, concat_axis=0, tiled=True)
    mixed = jnp.einsum(
        "hkp,hke->pe",
        attended,
        w_out.reshape(HEADS, head_dim, dec_width),
        preferred_element_type=jnp.float32,
    )
    return (mixed + dec_in.astype(jnp.float32)).astype(jnp.bfloat16)


def solution(mesh):
    placed = (
        P(("clip", "tok"), None),
        P(),
        P("tok", None, "clip"),
        P("tok", "clip", None),
        P(),
        P("clip", None),
        P(),
        P(),
        P(),
    )
    return jax.shard_map(
        per_device, mesh=mesh, in_specs=placed, out_specs=P(("clip", "tok"), None), check_vma=False
    )
```

profile of v0, /device:TPU:0, one launch (start us, length us, event | category | flops | bytes accessed | tf_op | source)
XLA Modules:
  0.0 457.1 jit_solution(16553922433638070908)
XLA Ops:
  9.8 2.6 fusion.59
  12.4 42.0 %pmax.7 = f32[1024]{0:T(1024)S(1)} all-reduce(f32[1024]{0:T(1024)S(1)} %get-tuple-element.46), channel_id=1, replica_groups=mesh['clip'=8,'tok'=16] {'tok'}, use_global_device_ids=true, to_apply=%region_5.0 | all-reduce | flops 1024 | bytes 8192 | tf_op jit(solution)/shard_map/pmax | solution.py:50
  54.5 5.0 %fusion.46 = f32[1024,1024]{1,0:T(8,128)} fusion(f32[512,1024]{1,0:T(8,128)} %get-tuple-element.70, f32[1024]{0:T(1024)S(1)} %pmax.7, bf16[512,1024]{1,0:T(8,128)(2,1)S(1)} %copy-done.1, f32[512]{0:T(512)S(1)} %add_rsqrt_fusion, f32[512]{0:T(512)S(1)} %broadcast_multiply_fusion), kind=kOutput, calls=%fused_computation.61 | convolution fusion | flops 1076887552 | bytes 7348224 | tf_op jit(solution)/shard_map/dot_general | solution.py:52
  61.3 2.3 fusion.13
  63.7 35.8 %all-reduce = f32[1024]{0:T(1024)S(1)} all-reduce(f32[1024]{0:T(1024)S(1)} %get-tuple-element.44), channel_id=3, replica_groups=mesh['clip'=8,'tok'=16] {'tok'}, use_global_device_ids=true, to_apply=%region_8.0.clone | all-reduce | flops 1024 | bytes 8192
  99.5 35.1 %reduce-scatter.3.cloned.1.call-done = f32[64,1024]{1,0:T(8,128)} async-done(((f32[1024,1024]{1,0:T(8,128)}), f32[64,1024]{1,0:T(8,128)}) %reduce-scatter.3.cloned.1.call-update) | async-done | bytes 262160 | tf_op jit(solution)/shard_map/reduce_scatter | solution.py:57
  136.3 22.4 %all-gather.4.cloned.1.call-done = bf16[512,1024]{1,0:T(8,128)(2,1)} async-done(((bf16[64,1024]{1,0:T(8,128)(2,1)}), bf16[512,1024]{1,0:T(8,128)(2,1)}) %all-gather.4.cloned.1.call-update) | async-done | bytes 1048592 | tf_op jit(solution)/shard_map/all_gather | solution.py:65
  158.7 4.6 %fusion.24 = f32[512,1024]{1,0:T(8,128)} fusion(bf16[1,512,1024]{2,1,0:T(8,128)(2,1)} %param.14, bf16[512,1024]{1,0:T(8,128)(2,1)} %all-gather.4.cloned.1.call-done, bf16[1,1024,512]{2,1,0:T(8,128)(2,1)} %param.13), kind=kOutput, calls=%fused_computation.39 | convolution fusion | flops 1076101120 | bytes 5242880 | tf_op jit(solution)/shard_map/dot_general | solution.py:70
  163.4 33.9 %reduce-scatter.5.cloned.1.call-done = f32[64,1024]{1,0:T(8,128)} async-done(((f32[512,1024]{1,0:T(8,128)}), f32[64,1024]{1,0:T(8,128)}) %reduce-scatter.5.cloned.1.call-update) | async-done | bytes 262160 | tf_op jit(solution)/shard_map/reduce_scatter | solution.py:71
  199.0 44.2 %all-gather.6.cloned.1.call-done = bf16[1024,1024]{1,0:T(8,128)(2,1)} async-done(((bf16[64,1024]{1,0:T(8,128)(2,1)}), bf16[1024,1024]{1,0:T(8,128)(2,1)}) %all-gather.6.cloned.1.call-update) | async-done | bytes 2097168 | tf_op jit(solution)/shard_map/all_gather | solution.py:79
  243.1 5.0 %convolution_convert_fusion.1 = bf16[512,512]{1,0:T(8,128)(2,1)} fusion(bf16[1024,512]{1,0:T(8,128)(2,1)S(1)} %copy-done.3, bf16[1024,1024]{1,0:T(8,128)(2,1)} %all-gather.6.cloned.1.call-done, f32[512,1024]{1,0:T(8,128)} %get-tuple-element.70, f32[512]{0:T(512)S(1)} %get-tuple-element.43, f32[512]{0:T(512)S(1)} %get-tuple-element.45), kind=kOutput, calls=%fused_computation.27 | convolution fusion | flops 1612972032 | bytes 5771264 | tf_op jit(solution)/shard_map/dot_general | solution.py:82
  250.6 67.9 %all-gather.8.cloned.1.call-done = bf16[8192,512]{1,0:T(8,128)(2,1)} async-done(((bf16[512,512]{1,0:T(8,128)(2,1)}), bf16[8192,512]{1,0:T(8,128)(2,1)}) %all-gather.8.cloned.1.call-update) | async-done | bytes 8388624 | tf_op jit(solution)/shard_map/all_gather | solution.py:94
  318.4 5.7 %gather_fusion = bf16[256,512]{1,0:T(8,128)(2,1)S(1)} fusion(bf16[8192,512]{1,0:T(8,128)(2,1)} %all-gather.8.cloned.1.call-done, s32[1024]{0:T(1024)S(1)} %pad_clamp_fusion), kind=kCustom, calls=%fused_computation | custom fusion | bytes 525312 | tf_op jit(solution)/shard_map/jit(_take)/gather | solution.py:95
  324.6 2.2 fusion.48
  327.9 5.3 %all-to-all-start = ((bf16[3,16,32,256]{3,2,0,1:T(8,128)(2,1)}), bf16[3,16,32,256]{3,2,0,1:T(8,128)(2,1)S(1)}, u32[]{:S(2)}, u32[]{:S(2)}) async-start(bf16[3,16,32,256]{3,2,0,1:T(8,128)(2,1)} %copy.19), calls=%async_computation.2 | async-start | bytes 1572864 | tf_op jit(solution)/shard_map/all_to_all | solution.py:105
  333.2 14.2 %all-to-all-done = bf16[3,16,32,256]{3,2,0,1:T(8,128)(2,1)S(1)} async-done(((bf16[3,16,32,256]{3,2,0,1:T(8,128)(2,1)}), bf16[3,16,32,256]{3,2,0,1:T(8,128)(2,1)S(1)}, u32[]{:S(2)}, u32[]{:S(2)}) %all-to-all-start) | async-done | bytes 786464 | tf_op jit(solution)/shard_map/all_to_all | solution.py:105
  350.6 48.1 %while.10 = (s32[]{:T(128)}, bf16[8,1,32,512]{3,2,1,0:T(8,128)(2,1)}, bf16[8,1,32,512]{3,2,1,0:T(8,128)(2,1)}, bf16[1,32,4096]{2,1,0:T(8,128)(2,1)S(1)}, bf16[1,32,4096]{2,1,0:T(8,128)(2,1)S(1)}, /*index=5*/s32[]{:T(128)}) while((s32[]{:T(128)}, bf16[8,1,32,512]{3,2,1,0:T(8,128)(2,1)}, bf16[8,1,32,512]{3,2,1,0:T(8,128)(2,1)}, ...), condition=%wide.region_15.16_spmd, body=%wide.region_12.15_spmd.sunk | while | flops 283147264 | bytes 25764932 | solution.py:40
  350.7 2.1 multiply_reduce_fusion.2
  356.7 2.1 multiply_reduce_fusion.2
  362.7 2.1 multiply_reduce_fusion.2
  368.7 2.1 multiply_reduce_fusion.2
  372.7 2.0 fusion.73
  374.7 2.1 multiply_reduce_fusion.2
  378.7 2.0 fusion.73
  380.7 2.1 multiply_reduce_fusion.2
  386.7 2.1 multiply_reduce_fusion.2
  392.7 2.1 multiply_reduce_fusion.2
  399.7 3.8 copy.25
  404.1 23.4 %reduce.6 = bf16[4096,32]{1,0:T(8,128)(2,1)S(1)} reduce(bf16[4096,1,32]{2,1,0:T(2,128)(2,1)} %bitcast.92, bf16[]{:T(256)} %broadcast.124), dimensions={1}, to_apply=%bitcast.67.reduce_sub_computation | reduce | bytes 524290
  429.2 12.0 %all_to_all.33 = bf16[16,2,4096]{2,1,0:T(2,128)(2,1)S(1)} all-to-all(bf16[16,2,4096]{2,1,0:T(2,128)(2,1)} %reshape.140), channel_id=1, replica_groups=mesh['clip'=8,'tok'=16] {'tok'}, dimensions={0} | all-to-all | bytes 524288 | tf_op jit(solution)/shard_map/all_to_all | solution.py:107
  441.2 3.6 reshape.141
  444.8 4.5 copy.26
  (72 shorter events, 46.8 us)
Async XLA Ops:
  6.5 3.2 copy-start
  6.5 3.3 copy-start.1
  6.5 128.0 %reduce-scatter.3.cloned.1.call-start = ((), (), s32[]{:S(2)}) async-start(), calls=%async_computation.4 | async-start | bytes 4456448 | tf_op jit(solution)/shard_map/reduce_scatter | solution.py:57
  59.5 0.7 copy-start.5
  59.5 99.2 %all-gather.4.cloned.1.call-start = ((), (), s32[]{:S(2)}) async-start(), calls=%async_computation.5 | async-start | bytes 1179648 | tf_op jit(solution)/shard_map/all_gather | solution.py:65
  136.3 61.0 %reduce-scatter.5.cloned.1.call-start = ((), (), s32[]{:S(2)}) async-start(), calls=%async_computation.6 | async-start | bytes 2359296 | tf_op jit(solution)/shard_map/reduce_scatter | solution.py:71
  163.3 79.8 %copy-start.3 = (bf16[1024,512]{1,0:T(8,128)(2,1)S(1)}, bf16[1024,512]{1,0:T(8,128)(2,1)}, u32[]{:S(2)}) copy-start(bf16[1024,512]{1,0:T(8,128)(2,1)} %param.15) | copy-start | bytes 3145732
  163.3 79.8 %all-gather.6.cloned.1.call-start = ((), (), s32[]{:S(2)}) async-start(), calls=%async_computation.7 | async-start | bytes 2228224 | tf_op jit(solution)/shard_map/all_gather | solution.py:79
  198.9 119.5 %all-gather.8.cloned.1.call-start = ((), (), s32[]{:S(2)}) async-start(), calls=%async_computation.8 | async-start | bytes 8912896 | tf_op jit(solution)/shard_map/all_gather | solution.py:94
  243.1 5.0 %copy-start.2 = (bf16[512]{0:T(512)(128)(2,1)S(1)}, bf16[512]{0:T(512)(128)(2,1)}, u32[]{:S(2)}) copy-start(bf16[512]{0:T(512)(128)(2,1)} %param.17) | copy-start | bytes 3076
  327.9 19.5 %all-to-all-start = ((bf16[3,16,32,256]{3,2,0,1:T(8,128)(2,1)}), bf16[3,16,32,256]{3,2,0,1:T(8,128)(2,1)S(1)}, u32[]{:S(2)}, u32[]{:S(2)}) async-start(bf16[3,16,32,256]{3,2,0,1:T(8,128)(2,1)} %copy.19), calls=%async_computation.2 | async-start | bytes 1572864 | tf_op jit(solution)/shard_map/all_to_all | solution.py:105
  441.2 8.2 %copy-start.4 = (bf16[512,512]{1,0:T(8,128)(2,1)S(1)}, bf16[512,512]{1,0:T(8,128)(2,1)}, u32[]{:S(2)}) copy-start(bf16[512,512]{1,0:T(8,128)(2,1)} %param.19) | copy-start | bytes 1572868
Sparse Core Ops, SparseCore 0:
  59.6 74.9 reduce-scatter.2
  136.4 22.2 all-gather.3
  163.5 33.7 reduce-scatter.4
  199.3 43.8 all-gather.5
  248.2 70.1 all-gather.7
where the time goes:
time: 458 us; the launch traced here: 457 us
  waiting for transfers between devices  218 us (48%)
  blocking collectives  89.8 us (20%)
  matrix products  53.5 us (12%)
  other arithmetic  50.5 us (11%)
  local copies, waits for them, and re-layouts  26.3 us (6%)
  between operations  14 us (3%)
  starting transfers between devices  5.47 us (1%)
    all_gather x1, waiting for transfers between devices, per_device(): everyone = lax.all_gather(projected, 'tok', axis=0, tiled=True)  67.9 us
    all_gather x1, waiting for transfers between devices, per_device(): lax.all_gather(slot_out, 'tok', axis=0, tiled=True)  44.2 us
    pmax x1, blocking collectives, per_device(): col_top = lax.pmax(jnp.max(logits, axis=0), 'tok')  42 us
    unnamed x1, blocking collectives  35.8 us
    reduce_scatter x1, waiting for transfers between devices, per_device(): lax.psum_scatter(slot_sums, 'tok', scatter_dimension=0, tiled=True)  35.1 us
    reduce_scatter x1, waiting for transfers between devices, per_device(): lax.psum_scatter(partial_out, 'clip', scatter_dimension=0, tiled=True)  33.9 us
    unnamed x1, other arithmetic  23.4 us
    all_gather x1, waiting for transfers between devices, per_device(): lax.all_gather(slot_in, 'clip', axis=0, tiled=True)  22.4 us
  transfers between devices with their start and end apart: 6, of which 6 were waited for; matrix products, arithmetic and copies ran while one was open for 1% of the time, Pallas kernels for 0%

commit v1 on v0

--- a/solution.py
+++ b/solution.py
@@ -91,7 +91,9 @@
     filler = (mask_token.astype(jnp.float32)[None, :] + sinusoid(places, dec_width)).astype(
         jnp.bfloat16
     )
-    everyone = lax.all_gather(projected, "tok", axis=0, tiled=True)
+    everyone = jnp.concatenate(
+        lax.all_to_all(jnp.stack([projected] * lax.axis_size("tok")), "tok", 0, 0), axis=0
+    )
     picked = jnp.take(everyone, jnp.minimum(own_list, vis_all - 1), axis=0)
     dec_in = jnp.where(visible[:, None], picked, filler)
     head_dim = dec_width // HEADS

time: 458 us -> 530 us (1.16)
  waiting for transfers between devices: 218 us -> 277 us
  starting transfers between devices: 5.47 us -> 13.8 us
    all_to_all x0 -> x1, waiting for transfers between devices: none -> 130 us  [per_device(): lax.all_to_all(jnp.stack([projected] * lax.axis_size('tok')), 'tok', 0, 0)]
    all_gather x1 -> x0, waiting for transfers between devices: 67.9 us -> none  [per_device(): everyone = lax.all_gather(projected, 'tok', axis=0, tiled=True)]
where the time goes in v1:
time: 530 us; the launch traced here: 528 us
  waiting for transfers between devices  277 us (52%)
  blocking collectives  89.8 us (17%)
  matrix products  52.9 us (10%)
  other arithmetic  50.5 us (10%)
  local copies, waits for them, and re-layouts  30.3 us (6%)
  between operations  14 us (3%)
  starting transfers between devices  13.8 us (3%)
    all_to_all x1, waiting for transfers between devices, per_device(): lax.all_to_all(jnp.stack([projected] * lax.axis_size('tok')), 'tok', 0, 0)  130 us
    all_gather x1, waiting for transfers between devices, per_device(): lax.all_gather(slot_out, 'tok', axis=0, tiled=True)  44.2 us
    pmax x1, blocking collectives, per_device(): col_top = lax.pmax(jnp.max(logits, axis=0), 'tok')  42 us
    unnamed x1, blocking collectives  35.8 us
    reduce_scatter x1, waiting for transfers between devices, per_device(): lax.psum_scatter(slot_sums, 'tok', scatter_dimension=0, tiled=True)  35.1 us
    reduce_scatter x1, waiting for transfers between devices, per_device(): lax.psum_scatter(partial_out, 'clip', scatter_dimension=0, tiled=True)  33.9 us
    unnamed x1, other arithmetic  23.4 us
    all_gather x1, waiting for transfers between devices, per_device(): lax.all_gather(slot_in, 'clip', axis=0, tiled=True)  22.4 us
  transfers between devices with their start and end apart: 6, of which 6 were waited for; matrix products, arithmetic and copies ran while one was open for 1% of the time, Pallas kernels for 0%

profile of v1, /device:TPU:0, one launch (start us, length us, event | category | flops | bytes accessed | tf_op | source)
XLA Modules:
  0.0 528.2 jit_solution(4204767585797317356)
XLA Ops:
  9.8 2.6 fusion.59
  12.4 42.0 %pmax.7 = f32[1024]{0:T(1024)S(1)} all-reduce(f32[1024]{0:T(1024)S(1)} %get-tuple-element.46), channel_id=1, replica_groups=mesh['clip'=8,'tok'=16] {'tok'}, use_global_device_ids=true, to_apply=%region_5.0 | all-reduce | flops 1024 | bytes 8192 | tf_op jit(solution)/shard_map/pmax | solution.py:50
  54.5 5.0 fusion.46
  61.3 2.3 fusion.13
  63.7 35.8 %all-reduce = f32[1024]{0:T(1024)S(1)} all-reduce(f32[1024]{0:T(1024)S(1)} %get-tuple-element.44), channel_id=3, replica_groups=mesh['clip'=8,'tok'=16] {'tok'}, use_global_device_ids=true, to_apply=%region_8.0.clone | all-reduce | flops 1024 | bytes 8192
  99.5 35.1 %reduce-scatter.3.cloned.1.call-done = f32[64,1024]{1,0:T(8,128)} async-done(((f32[1024,1024]{1,0:T(8,128)}), f32[64,1024]{1,0:T(8,128)}) %reduce-scatter.3.cloned.1.call-update) | async-done | bytes 262160 | tf_op jit(solution)/shard_map/reduce_scatter | solution.py:57
  136.3 22.4 %all-gather.3.cloned.1.call-done = bf16[512,1024]{1,0:T(8,128)(2,1)} async-done(((bf16[64,1024]{1,0:T(8,128)(2,1)}), bf16[512,1024]{1,0:T(8,128)(2,1)}) %all-gather.3.cloned.1.call-update) | async-done | bytes 1048592 | tf_op jit(solution)/shard_map/all_gather | solution.py:65
  158.7 4.6 fusion.24
  163.4 33.9 %reduce-scatter.5.cloned.1.call-done = f32[64,1024]{1,0:T(8,128)} async-done(((f32[512,1024]{1,0:T(8,128)}), f32[64,1024]{1,0:T(8,128)}) %reduce-scatter.5.cloned.1.call-update) | async-done | bytes 262160 | tf_op jit(solution)/shard_map/reduce_scatter | solution.py:71
  198.9 44.2 %all-gather.5.cloned.1.call-done = bf16[1024,1024]{1,0:T(8,128)(2,1)} async-done(((bf16[64,1024]{1,0:T(8,128)(2,1)}), bf16[1024,1024]{1,0:T(8,128)(2,1)}) %all-gather.5.cloned.1.call-update) | async-done | bytes 2097168 | tf_op jit(solution)/shard_map/all_gather | solution.py:79
  243.1 4.4 convolution_convert_fusion.1
  247.5 4.0 stack.2
  251.5 5.1 all-to-all-start
  259.1 129.7 %all-to-all-done = bf16[16,512,512]{2,1,0:T(8,128)(2,1)} async-done(((bf16[16,512,512]{2,1,0:T(8,128)(2,1)}), bf16[16,512,512]{2,1,0:T(8,128)(2,1)}, u32[]{:S(2)}, u32[]{:S(2)}) %all-to-all-start) | async-done | bytes 8388640 | tf_op jit(solution)/shard_map/all_to_all | solution.py:95
  388.8 5.7 %gather_fusion = bf16[256,512]{1,0:T(8,128)(2,1)S(1)} fusion(bf16[8192,512]{1,0:T(8,128)(2,1)} %bitcast.8, s32[1024]{0:T(1024)S(1)} %pad_clamp_fusion), kind=kCustom, calls=%fused_computation | custom fusion | bytes 525312 | tf_op jit(solution)/shard_map/jit(_take)/gather | solution.py:97
  395.0 2.2 fusion.48
  398.3 8.6 %all-to-all-start.1 = ((bf16[3,16,32,256]{3,2,0,1:T(8,128)(2,1)}), bf16[3,16,32,256]{3,2,0,1:T(8,128)(2,1)S(1)}, u32[]{:S(2)}, u32[]{:S(2)}) async-start(bf16[3,16,32,256]{3,2,0,1:T(8,128)(2,1)} %copy.19), calls=%async_computation.3 | async-start | bytes 1572864 | tf_op jit(solution)/shard_map/all_to_all | solution.py:107
  406.9 11.5 %all-to-all-done.1 = bf16[3,16,32,256]{3,2,0,1:T(8,128)(2,1)S(1)} async-done(((bf16[3,16,32,256]{3,2,0,1:T(8,128)(2,1)}), bf16[3,16,32,256]{3,2,0,1:T(8,128)(2,1)S(1)}, u32[]{:S(2)}, u32[]{:S(2)}) %all-to-all-start.1) | async-done | bytes 786464 | tf_op jit(solution)/shard_map/all_to_all | solution.py:107
  421.6 48.1 %while.10 = (s32[]{:T(128)}, bf16[8,1,32,512]{3,2,1,0:T(8,128)(2,1)}, bf16[8,1,32,512]{3,2,1,0:T(8,128)(2,1)}, bf16[1,32,4096]{2,1,0:T(8,128)(2,1)S(1)}, bf16[1,32,4096]{2,1,0:T(8,128)(2,1)S(1)}, /*index=5*/s32[]{:T(128)}) while((s32[]{:T(128)}, bf16[8,1,32,512]{3,2,1,0:T(8,128)(2,1)}, bf16[8,1,32,512]{3,2,1,0:T(8,128)(2,1)}, ...), condition=%wide.region_15.16_spmd, body=%wide.region_12.15_spmd.sunk | while | flops 283147264 | bytes 25764932 | solution.py:40
  421.7 2.1 multiply_reduce_fusion.2
  427.7 2.1 multiply_reduce_fusion.2
  433.7 2.1 multiply_reduce_fusion.2
  439.7 2.1 multiply_reduce_fusion.2
  445.7 2.1 multiply_reduce_fusion.2
  451.7 2.1 multiply_reduce_fusion.2
  457.7 2.1 multiply_reduce_fusion.2
  463.7 2.1 multiply_reduce_fusion.2
  470.7 3.8 copy.25
  475.1 23.4 %reduce.6 = bf16[4096,32]{1,0:T(8,128)(2,1)S(1)} reduce(bf16[4096,1,32]{2,1,0:T(2,128)(2,1)} %bitcast.93, bf16[]{:T(256)} %broadcast.126), dimensions={1}, to_apply=%bitcast.68.reduce_sub_computation | reduce | bytes 524290
  500.2 12.0 %all_to_all.38 = bf16[16,2,4096]{2,1,0:T(2,128)(2,1)S(1)} all-to-all(bf16[16,2,4096]{2,1,0:T(2,128)(2,1)} %reshape.146), channel_id=1, replica_groups=mesh['clip'=8,'tok'=16] {'tok'}, dimensions={0} | all-to-all | bytes 524288 | tf_op jit(solution)/shard_map/all_to_all | solution.py:109
  512.2 3.6 reshape.147
  515.9 4.5 copy.26
  (70 shorter events, 50.7 us)
Async XLA Ops:
  6.5 3.2 copy-start
  6.5 3.3 copy-start.1
  6.5 128.0 %reduce-scatter.3.cloned.1.call-start = ((), (), s32[]{:S(2)}) async-start(), calls=%async_computation.5 | async-start | bytes 4456448 | tf_op jit(solution)/shard_map/reduce_scatter | solution.py:57
  59.5 0.7 copy-start.4
  59.5 99.2 %all-gather.3.cloned.1.call-start = ((), (), s32[]{:S(2)}) async-start(), calls=%async_computation.6 | async-start | bytes 1179648 | tf_op jit(solution)/shard_map/all_gather | solution.py:65
  136.3 61.0 %reduce-scatter.5.cloned.1.call-start = ((), (), s32[]{:S(2)}) async-start(), calls=%async_computation.7 | async-start | bytes 2359296 | tf_op jit(solution)/shard_map/reduce_scatter | solution.py:71
  163.3 79.8 %all-gather.5.cloned.1.call-start = ((), (), s32[]{:S(2)}) async-start(), calls=%async_computation.8 | async-start | bytes 2228224 | tf_op jit(solution)/shard_map/all_gather | solution.py:79
  251.5 5.1 copy-start.2
  251.5 137.3 %all-to-all-start = ((bf16[16,512,512]{2,1,0:T(8,128)(2,1)}), bf16[16,512,512]{2,1,0:T(8,128)(2,1)}, u32[]{:S(2)}, u32[]{:S(2)}) async-start(bf16[16,512,512]{2,1,0:T(8,128)(2,1)} %stack.2), calls=%async_computation.2 | async-start | bytes 16777216 | tf_op jit(solution)/shard_map/all_to_all | solution.py:95
  398.3 20.1 %all-to-all-start.1 = ((bf16[3,16,32,256]{3,2,0,1:T(8,128)(2,1)}), bf16[3,16,32,256]{3,2,0,1:T(8,128)(2,1)S(1)}, u32[]{:S(2)}, u32[]{:S(2)}) async-start(bf16[3,16,32,256]{3,2,0,1:T(8,128)(2,1)} %copy.19), calls=%async_computation.3 | async-start | bytes 1572864 | tf_op jit(solution)/shard_map/all_to_all | solution.py:107
  512.2 8.2 %copy-start.3 = (bf16[512,512]{1,0:T(8,128)(2,1)S(1)}, bf16[512,512]{1,0:T(8,128)(2,1)}, u32[]{:S(2)}) copy-start(bf16[512,512]{1,0:T(8,128)(2,1)} %param.19) | copy-start | bytes 1572868
Sparse Core Ops, SparseCore 0:
  59.6 74.9 reduce-scatter.2
  136.4 22.2 all-gather.2
  163.5 33.7 reduce-scatter.4
  199.3 43.8 all-gather.4
